TPU v7x, 32 devices: a whole 2x2x4 slice. The times are simulated.
32 devices in a mesh: layer: 4 (over x, core), grid: 8 (over z, y).
Axes of the slice: x: 2, y: 2, z: 4, core: 2. Of those that a mesh axis runs over, the one named last changes fastest.
Arguments:
- band_blocks: bfloat16 [80, 9, 128, 128], P('grid'), may hold values from -7 to 7, as said below
- retained: int32 [80, 9], P('grid'), may hold values from 0 to 1, as said below
Outputs:
- purified: bfloat16 [80, 9, 128, 128], P('grid', None, 'layer')
Inputs may be any that keep to these rules, and one draw needn't show every extreme that they name: `band_blocks`: the matrix is symmetric: block slot w of block row i equals the transpose of block slot 8 - w of block row (i + w - 4) mod 80. retained[i, w] = 1 exactly when retained[(i + w - 4) mod 80, 8 - w] = 1; the middle slot w = 4 is 1 in every block row.
All inputs are finite; a program needn't handle non-finite values.
Results may differ from a plain program's by a relative error of at most 0.005.
Values may be sent and summed in bfloat16 or wider, within the bound.
A program may use at most 64 MiB of HBM per device.

v0:
```python
import jax
import jax.numpy as jnp
from jax import lax
from jax.sharding import PartitionSpec as P

STEPS = 2


def extended(block, sides, width):
    for axis, dim in sides:
        count = lax.axis_size(axis)
        forward = [(i, i + 1) for i in range(count - 1)]
        forward.append((count - 1, 0))
        backward = [(target, source) for source, target in forward]
        low = lax.ppermute(
            lax.slice_in_dim(block, block.shape[dim] - width, None, axis=dim), axis, forward
        )
        high = lax.ppermute(lax.slice_in_dim(block, 0, width, axis=dim), axis, backward)
        block = jnp.concatenate([low, block, high], axis=dim)
    return block


def strip_product(left_rows, halo_rows, reach):
    row_count = left_rows.shape[0]
    band_width = left_rows.shape[1]
    padded = jnp.pad(halo_rows, ((0, 0), (reach, reach), (0, 0), (0, 0)))
    running = jnp.zeros(
        (row_count, band_width, left_rows.shape[2], halo_rows.shape[3]), jnp.float32
    )
    for offset in range(band_width):
        source = padded[
            offset : offset + row_count, 2 * reach - offset : 2 * reach - offset + band_width
        ]
        running = running + jnp.einsum(
            "rab,rwbc->rwac", left_rows[:, offset], source, preferred_element_type=jnp.float32
        )
    return running


def per_device(band_blocks, retained):
    layer_count = lax.axis_size("layer")
    share = lax.axis_index("layer")
    band_width = band_blocks.shape[1]
    block_width = band_blocks.shape[2]
    reach = (band_width - 1) // 2
    piece = block_width // layer_count
    kept = (retained != 0)[:, :, None, None]
    whole_rows = jnp.where(kept, band_blocks, jnp.zeros_like(band_blocks))
    quarter = lax.dynamic_slice_in_dim(whole_rows, share * piece, piece, 2)
    for repeat in range(STEPS):
        halo_part = extended(quarter, (("grid", 0),), reach)
        halo_rows = lax.all_gather(halo_part, "layer", axis=2, tiled=True)
        square = jnp.where(kept, strip_product(quarter, halo_rows, reach), 0.0).astype(jnp.bfloat16)
        cube = jnp.where(kept, strip_product(square, halo_rows, reach), 0.0)
        quarter = (
            (3.0 * quarter.astype(jnp.float32) - cube / (4.0 * band_width * block_width)) * 0.5
        ).astype(jnp.bfloat16)
    return quarter


def solution(mesh):
    return jax.shard_map(
        per_device,
        mesh=mesh,
        in_specs=(P("grid", None, None, None), P("grid", None)),
        out_specs=P("grid", None, "layer", None),
        check_vma=False,
    )
```

profile of v0, /device:TPU:0, one launch (start us, length us, event | category | flops | bytes accessed | tf_op | source)
XLA Modules:
  0.0 161.0 jit_solution(15024510150904314228)
XLA Ops:
  6.5 0.9 broadcast_compare_fusion
  7.5 0.9 copy-done
  8.7 3.0 %collective-permute-start = (bf16[4,9,32,128]{3,2,0,1:T(8,128)(2,1)S(1)}, bf16[4,9,32,128]{3,2,0,1:T(8,128)(2,1)S(1)}, u32[]{:S(2)}, u32[]{:S(2)}) collective-permute-start(bf16[4,9,32,128]{3,2,0,1:T(8,128)(2,1)S(1)} %get-tuple-element.7), channel_id=1, source_target_pairs={{0,1},{1,2},{2,3},{3,4},{4,5},{5,6},{6,7},{7,0},{8,9},{9,10},{10,1... | collective-permute-start | bytes 884744 | tf_op jit(solution)/shard_map/ppermute | solution.py:15
  11.7 3.1 %collective-permute-start.1 = (bf16[4,9,32,128]{3,2,0,1:T(8,128)(2,1)S(1)}, bf16[4,9,32,128]{3,2,0,1:T(8,128)(2,1)S(1)}, u32[]{:S(2)}, u32[]{:S(2)}) collective-permute-start(bf16[4,9,32,128]{3,2,0,1:T(8,128)(2,1)S(1)} %get-tuple-element.8), channel_id=1, source_target_pairs={{1,0},{2,1},{3,2},{4,3},{5,4},{6,5},{7,6},{0,7},{9,8},{10,9},{11,1... | collective-permute-start | bytes 884744 | tf_op jit(solution)/shard_map/ppermute | solution.py:18
  14.8 9.5 %collective-permute-done = bf16[4,9,32,128]{3,2,0,1:T(8,128)(2,1)S(1)} collective-permute-done((bf16[4,9,32,128]{3,2,0,1:T(8,128)(2,1)S(1)}, bf16[4,9,32,128]{3,2,0,1:T(8,128)(2,1)S(1)}, u32[]{:S(2)}, u32[]{:S(2)}) %collective-permute-start) | collective-permute-done | bytes 294944 | tf_op jit(solution)/shard_map/ppermute | solution.py:15
  24.3 2.2 %collective-permute-done.1 = bf16[4,9,32,128]{3,2,0,1:T(8,128)(2,1)S(1)} collective-permute-done((bf16[4,9,32,128]{3,2,0,1:T(8,128)(2,1)S(1)}, bf16[4,9,32,128]{3,2,0,1:T(8,128)(2,1)S(1)}, u32[]{:S(2)}, u32[]{:S(2)}) %collective-permute-start.1) | collective-permute-done | bytes 294944 | tf_op jit(solution)/shard_map/ppermute | solution.py:18
  26.5 1.3 pad_maximum_fusion
  27.8 40.9 %all-gather.3.cloned.1.call-done = bf16[18,9,128,128]{3,2,0,1:T(8,128)(2,1)} async-done(((bf16[18,9,32,128]{3,2,0,1:T(8,128)(2,1)}), bf16[18,9,128,128]{3,2,0,1:T(8,128)(2,1)}) %all-gather.3.cloned.1.call-update) | async-done | bytes 5308432 | tf_op jit(solution)/shard_map/all_gather | solution.py:52
  68.7 2.2 %fusion.24 = f32[10,9,128,32]{2,3,0,1:T(8,128)S(1)} fusion(bf16[18,9,128,128]{3,2,0,1:T(8,128)(2,1)} %all-gather.3.cloned.1.call-done, bf16[10,9,32,128]{3,2,0,1:T(8,128)(2,1)} %copy-done.7), kind=kOutput, calls=%fused_computation.44 | convolution fusion | flops 94371840 | bytes 6864896 | tf_op jit(solution)/shard_map/rab,rwbc->rwac/dot_general | solution.py:34
  71.0 0.9 copy-done.2
  72.5 0.6 fusion.20
  73.1 0.6 fusion.18
  75.7 0.9 fusion.40
  77.5 0.6 fusion.21
  78.1 0.6 fusion.6
  78.7 0.6 fusion.19
  80.7 1.1 fusion.11
  81.9 1.5 collective-permute-start.2
  83.4 3.3 %collective-permute-start.3 = (bf16[4,9,32,128]{3,2,0,1:T(8,128)(2,1)S(1)}, bf16[4,9,32,128]{3,2,0,1:T(8,128)(2,1)S(1)}, u32[]{:S(2)}, u32[]{:S(2)}) collective-permute-start(bf16[4,9,32,128]{3,2,0,1:T(8,128)(2,1)S(1)} %get-tuple-element.6), channel_id=1, source_target_pairs={{1,0},{2,1},{3,2},{4,3},{5,4},{6,5},{7,6},{0,7},{9,8},{10,9},{11,1... | collective-permute-start | bytes 884744 | tf_op jit(solution)/shard_map/ppermute | solution.py:18
  86.7 9.8 %collective-permute-done.2 = bf16[4,9,32,128]{3,2,0,1:T(8,128)(2,1)S(1)} collective-permute-done((bf16[4,9,32,128]{3,2,0,1:T(8,128)(2,1)S(1)}, bf16[4,9,32,128]{3,2,0,1:T(8,128)(2,1)S(1)}, u32[]{:S(2)}, u32[]{:S(2)}) %collective-permute-start.2) | collective-permute-done | bytes 294944 | tf_op jit(solution)/shard_map/ppermute | solution.py:15
  96.4 2.2 %collective-permute-done.3 = bf16[4,9,32,128]{3,2,0,1:T(8,128)(2,1)S(1)} collective-permute-done((bf16[4,9,32,128]{3,2,0,1:T(8,128)(2,1)S(1)}, bf16[4,9,32,128]{3,2,0,1:T(8,128)(2,1)S(1)}, u32[]{:S(2)}, u32[]{:S(2)}) %collective-permute-start.3) | collective-permute-done | bytes 294944 | tf_op jit(solution)/shard_map/ppermute | solution.py:18
  98.6 1.3 pad_maximum_fusion.1
  99.9 39.7 %all-gather.5.cloned.1.call-done = bf16[18,9,128,128]{3,2,0,1:T(8,128)(2,1)} async-done(((bf16[18,9,32,128]{3,2,0,1:T(8,128)(2,1)}), bf16[18,9,128,128]{3,2,0,1:T(8,128)(2,1)}) %all-gather.5.cloned.1.call-update) | async-done | bytes 5308432 | tf_op jit(solution)/shard_map/all_gather | solution.py:52
  139.7 2.2 %fusion.38 = f32[10,9,128,32]{2,3,0,1:T(8,128)S(1)} fusion(bf16[18,9,128,128]{3,2,0,1:T(8,128)(2,1)} %all-gather.5.cloned.1.call-done, bf16[10,9,32,128]{3,2,0,1:T(8,128)(2,1)} %copy-done.4), kind=kOutput, calls=%fused_computation.58 | convolution fusion | flops 94371840 | bytes 6864896 | tf_op jit(solution)/shard_map/rab,rwbc->rwac/dot_general | solution.py:34
  141.9 0.9 copy-done.3
  143.8 0.6 fusion.32
  146.4 1.0 fusion.41
  149.0 0.6 fusion.2
  149.5 0.6 fusion.33
  151.6 0.6 copy-done.6
  152.2 1.0 fusion.9
  153.2 0.9 copy.78
  (44 shorter events, 11.7 us)
Async XLA Ops:
  6.5 1.8 %copy-start = (bf16[10,9,128,128]{3,2,1,0:T(8,128)(2,1)S(1)}, bf16[10,9,128,128]{3,2,1,0:T(8,128)(2,1)}, u32[]{:S(2)}) copy-start(bf16[10,9,128,128]{3,2,1,0:T(8,128)(2,1)} %param.2) | copy-start | bytes 8847364
  6.5 62.2 %all-gather.3.cloned.1.call-start = ((), (), s32[]{:S(2)}) async-start(), calls=%async_computation | async-start | bytes 6635520 | tf_op jit(solution)/shard_map/all_gather | solution.py:52
  8.6 17.9 %copy-start.7 = (bf16[10,9,32,128]{3,2,0,1:T(8,128)(2,1)}, bf16[10,9,32,128]{3,2,0,1:T(8,128)(2,1)S(1)}, u32[]{:S(2)}) copy-start(bf16[10,9,32,128]{3,2,0,1:T(8,128)(2,1)S(1)} %copy_select_fusion) | copy-start | bytes 2211844
  8.7 15.6 %collective-permute-start = (bf16[4,9,32,128]{3,2,0,1:T(8,128)(2,1)S(1)}, bf16[4,9,32,128]{3,2,0,1:T(8,128)(2,1)S(1)}, u32[]{:S(2)}, u32[]{:S(2)}) collective-permute-start(bf16[4,9,32,128]{3,2,0,1:T(8,128)(2,1)S(1)} %get-tuple-element.7), channel_id=1, source_target_pairs={{0,1},{1,2},{2,3},{3,4},{4,5},{5,6},{6,7},{7,0},{8,9},{9,10},{10,1... | collective-permute-start | bytes 884744 | tf_op jit(solution)/shard_map/ppermute | solution.py:15
  11.7 14.8 %collective-permute-start.1 = (bf16[4,9,32,128]{3,2,0,1:T(8,128)(2,1)S(1)}, bf16[4,9,32,128]{3,2,0,1:T(8,128)(2,1)S(1)}, u32[]{:S(2)}, u32[]{:S(2)}) collective-permute-start(bf16[4,9,32,128]{3,2,0,1:T(8,128)(2,1)S(1)} %get-tuple-element.8), channel_id=1, source_target_pairs={{1,0},{2,1},{3,2},{4,3},{5,4},{6,5},{7,6},{0,7},{9,8},{10,9},{11,1... | collective-permute-start | bytes 884744 | tf_op jit(solution)/shard_map/ppermute | solution.py:18
  27.8 111.9 %all-gather.5.cloned.1.call-start = ((), (), s32[]{:S(2)}) async-start(), calls=%async_computation.1 | async-start | bytes 6635520 | tf_op jit(solution)/shard_map/all_gather | solution.py:52
  68.7 3.1 %copy-start.2 = (bf16[18,9,128,128]{3,2,0,1:T(8,128)(2,1)S(1)}, bf16[18,9,128,128]{3,2,0,1:T(8,128)(2,1)}, u32[]{:S(2)}) copy-start(bf16[18,9,128,128]{3,2,0,1:T(8,128)(2,1)} %all-gather.3.cloned.1.call-done) | copy-start | bytes 15925252
  68.7 3.3 %copy-start.8 = (bf16[10,9,32,128]{3,2,0,1:T(8,128)(2,1)S(1)}, bf16[10,9,32,128]{3,2,0,1:T(8,128)(2,1)}, u32[]{:S(2)}) copy-start(bf16[10,9,32,128]{3,2,0,1:T(8,128)(2,1)} %copy-done.7) | copy-start | bytes 2211844
  81.8 16.8 %copy-start.4 = (bf16[10,9,32,128]{3,2,0,1:T(8,128)(2,1)}, bf16[10,9,32,128]{3,2,0,1:T(8,128)(2,1)S(1)}, u32[]{:S(2)}) copy-start(bf16[10,9,32,128]{3,2,0,1:T(8,128)(2,1)S(1)} %fusion.11) | copy-start | bytes 2211844
  81.9 14.5 %collective-permute-start.2 = (bf16[4,9,32,128]{3,2,0,1:T(8,128)(2,1)S(1)}, bf16[4,9,32,128]{3,2,0,1:T(8,128)(2,1)S(1)}, u32[]{:S(2)}, u32[]{:S(2)}) collective-permute-start(bf16[4,9,32,128]{3,2,0,1:T(8,128)(2,1)S(1)} %get-tuple-element.5), channel_id=1, source_target_pairs={{0,1},{1,2},{2,3},{3,4},{4,5},{5,6},{6,7},{7,0},{8,9},{9,10},{10,1... | collective-permute-start | bytes 884744 | tf_op jit(solution)/shard_map/ppermute | solution.py:15
  83.4 15.2 %collective-permute-start.3 = (bf16[4,9,32,128]{3,2,0,1:T(8,128)(2,1)S(1)}, bf16[4,9,32,128]{3,2,0,1:T(8,128)(2,1)S(1)}, u32[]{:S(2)}, u32[]{:S(2)}) collective-permute-start(bf16[4,9,32,128]{3,2,0,1:T(8,128)(2,1)S(1)} %get-tuple-element.6), channel_id=1, source_target_pairs={{1,0},{2,1},{3,2},{4,3},{5,4},{6,5},{7,6},{0,7},{9,8},{10,9},{11,1... | collective-permute-start | bytes 884744 | tf_op jit(solution)/shard_map/ppermute | solution.py:18
  99.9 42.0 %copy-start.5 = (bf16[10,9,32,128]{3,2,0,1:T(8,128)(2,1)S(1)}, bf16[10,9,32,128]{3,2,0,1:T(8,128)(2,1)}, u32[]{:S(2)}) copy-start(bf16[10,9,32,128]{3,2,0,1:T(8,128)(2,1)} %copy-done.4) | copy-start | bytes 2211844
  139.7 3.1 %copy-start.3 = (bf16[18,9,128,128]{3,2,0,1:T(8,128)(2,1)S(1)}, bf16[18,9,128,128]{3,2,0,1:T(8,128)(2,1)}, u32[]{:S(2)}) copy-start(bf16[18,9,128,128]{3,2,0,1:T(8,128)(2,1)} %all-gather.5.cloned.1.call-done) | copy-start | bytes 15925252
  151.1 1.1 copy-start.6
  152.2 1.9 %copy-start.1 = (bf16[10,9,128,128]{3,2,1,0:T(8,128)(2,1)S(1)}, bf16[10,9,128,128]{3,2,1,0:T(8,128)(2,1)}, u32[]{:S(2)}) copy-start(bf16[10,9,128,128]{3,2,1,0:T(8,128)(2,1)} %param.2) | copy-start | bytes 8847364
Sparse Core Ops, SparseCore 0:
  27.9 40.7 all-gather.2
  100.0 39.5 all-gather.4
where the time goes:
time: 161 us
  waiting for transfers between devices  104 us (65%)
  matrix products  23.9 us (15%)
  between operations  13.6 us (8%)
  starting transfers between devices  11 us (7%)
  local copies, waits for them, and re-layouts  4.62 us (3%)
  other arithmetic  3.59 us (2%)
    all_gather x2, waiting for transfers between devices, per_device(): halo_rows = lax.all_gather(halo_part, 'layer', axis=2, tiled=True)  80.6 us
    dot_general x36, matrix products, strip_product(): jnp.einsum('rab,rwbc->rwac', left_rows[:, offset], source, preferred_elem...  23.9 us
    ppermute x2, waiting for transfers between devices, extended(): lax.ppermute(lax.slice_in_dim(block, block.shape[dim] - width, None, axis...  19.2 us
    ppermute x2, starting transfers between devices, extended(): lax.ppermute(lax.slice_in_dim(block, 0, width, axis=dim), axis, backward)  6.36 us
    ppermute x2, starting transfers between devices, extended(): lax.ppermute(lax.slice_in_dim(block, block.shape[dim] - width, None, axis...  4.57 us
    ppermute x2, waiting for transfers between devices, extended(): lax.ppermute(lax.slice_in_dim(block, 0, width, axis=dim), axis, backward)  4.4 us
    unnamed x18, local copies, waits for them, and re-layouts  3.52 us
  transfers between devices with their start and end apart: 6, of which 6 were waited for; matrix products, arithmetic and copies ran while one was open for 0% of the time, Pallas kernels for 0%

commit v1 on v0

--- a/solution.py
+++ b/solution.py
@@ -49,7 +49,24 @@
     quarter = lax.dynamic_slice_in_dim(whole_rows, share * piece, piece, 2)
     for repeat in range(STEPS):
         halo_part = extended(quarter, (("grid", 0),), reach)
-        halo_rows = lax.all_gather(halo_part, "layer", axis=2, tiled=True)
+        ways, here, step = (lax.axis_size("layer"), lax.axis_index("layer"), halo_part.shape[2])
+        shape = [n * ways if d == 2 else n for d, n in enumerate(halo_part.shape)]
+        halo_rows = lax.dynamic_update_slice_in_dim(
+            jnp.zeros(shape, halo_part.dtype), halo_part, here * step, axis=2
+        )
+        going_up = going_down = halo_part
+        for far in range(1, ways // 2 + 1):
+            going_up = lax.ppermute(going_up, "layer", [(d, (d + 1) % ways) for d in range(ways)])
+            halo_rows = lax.dynamic_update_slice_in_dim(
+                halo_rows, going_up, (here - far) % ways * step, axis=2
+            )
+            if 2 * far < ways:
+                going_down = lax.ppermute(
+                    going_down, "layer", [(d, (d - 1) % ways) for d in range(ways)]
+                )
+                halo_rows = lax.dynamic_update_slice_in_dim(
+                    halo_rows, going_down, (here + far) % ways * step, axis=2
+                )
         square = jnp.where(kept, strip_product(quarter, halo_rows, reach), 0.0).astype(jnp.bfloat16)
         cube = jnp.where(kept, strip_product(square, halo_rows, reach), 0.0)
         quarter = (

time: 161 us -> 195 us (1.21)
  local copies, waits for them, and re-layouts: 4.62 us -> 28.5 us
  matrix products: 23.9 us -> 40.6 us
  between operations: 13.6 us -> 0.23 us
  waiting for transfers between devices: 104 us -> 108 us
  starting transfers between devices: 11 us -> 14.5 us
    ppermute x0 -> x6, waiting for transfers between devices: none -> 85 us  [the longest x4 85 us: per_device(): lax.ppermute(going_up, 'layer', [(d, (d + 1) % ways) for d in range(ways)])]
    all_gather x2 -> x0, waiting for transfers between devices: 80.6 us -> none  [per_device(): halo_rows = lax.all_gather(halo_part, 'layer', axis=2, tiled=True)]
    slice x0 -> x2, local copies, waits for them, and re-layouts: none -> 17.2 us  [strip_product(): padded[offset:offset + row_count, 2 * reach - offset:2 * reach - offset +...]
    dot_general x36, matrix products: 23.9 us -> 40.6 us  [strip_product(): jnp.einsum('rab,rwbc->rwac', left_rows[:, offset], source, preferred_elem...]
    dynamic_update_slice x0 -> x6, local copies, waits for them, and re-layouts: none -> 5.95 us  [the longest x4 3.96 us: per_device(): lax.dynamic_update_slice_in_dim(halo_rows, going_up, (here - far) % ways...]
    ppermute x0 -> x6, starting transfers between devices: none -> 3.62 us  [the longest x2 3.48 us: per_device(): lax.ppermute(going_down, 'layer', [(d, (d - 1) % ways) for d in range(way...]
    another operation x0 -> x2, local copies, waits for them, and re-layouts: none -> 2.64 us
  transfers between devices with their start and end apart: 6 -> 10, of which waited for: 6 -> 8; matrix products, arithmetic and copies ran while one was open for 0% -> 4% of each run, Pallas kernels for 0% -> 0%
where the time goes in v1:
time: 195 us
  waiting for transfers between devices  108 us (55%)
  matrix products  40.6 us (21%)
  local copies, waits for them, and re-layouts  28.5 us (15%)
  starting transfers between devices  14.5 us (7%)
  other arithmetic  3.11 us (2%)
    ppermute x4, waiting for transfers between devices, per_device(): lax.ppermute(going_up, 'layer', [(d, (d + 1) % ways) for d in range(ways)])  85 us
    dot_general x36, matrix products, strip_product(): jnp.einsum('rab,rwbc->rwac', left_rows[:, offset], source, preferred_elem...  40.6 us
    ppermute x2, waiting for transfers between devices, extended(): lax.ppermute(lax.slice_in_dim(block, block.shape[dim] - width, None, axis...  17.9 us
    slice x2, local copies, waits for them, and re-layouts, strip_product(): padded[offset:offset + row_count, 2 * reach - offset:2 * reach - offset +...  17.2 us
    ppermute x2, starting transfers between devices, extended(): lax.ppermute(lax.slice_in_dim(block, 0, width, axis=dim), axis, backward)  7.55 us
    ppermute x2, waiting for transfers between devices, extended(): lax.ppermute(lax.slice_in_dim(block, 0, width, axis=dim), axis, backward)  5.07 us
    dynamic_update_slice x4, local copies, waits for them, and re-layouts, per_device(): lax.dynamic_update_slice_in_dim(halo_rows, going_up, (here - far) % ways...  3.96 us
  transfers between devices with their start and end apart: 10, of which 8 were waited for; matrix products, arithmetic and copies ran while one was open for 4% of the time, Pallas kernels for 0%

profile of v1, /device:TPU:0, one launch (start us, length us, event | category | flops | bytes accessed | tf_op | source)
XLA Modules:
  0.0 194.9 jit_solution(9540432226506608698)
XLA Ops:
  2.1 3.0 %collective-permute-start = (bf16[4,9,32,128]{3,2,0,1:T(8,128)(2,1)S(1)}, bf16[4,9,32,128]{3,2,0,1:T(8,128)(2,1)S(1)}, u32[]{:S(2)}, u32[]{:S(2)}) collective-permute-start(bf16[4,9,32,128]{3,2,0,1:T(8,128)(2,1)S(1)} %get-tuple-element.25), channel_id=1, source_target_pairs={{0,1},{1,2},{2,3},{3,4},{4,5},{5,6},{6,7},{7,0},{8,9},{9,10},{10,1... | collective-permute-start | bytes 884744 | tf_op jit(solution)/shard_map/ppermute | solution.py:15
  5.2 3.1 %collective-permute-start.1 = (bf16[4,9,32,128]{3,2,0,1:T(8,128)(2,1)S(1)}, bf16[4,9,32,128]{3,2,0,1:T(8,128)(2,1)S(1)}, u32[]{:S(2)}, u32[]{:S(2)}) collective-permute-start(bf16[4,9,32,128]{3,2,0,1:T(8,128)(2,1)S(1)} %get-tuple-element.26), channel_id=1, source_target_pairs={{1,0},{2,1},{3,2},{4,3},{5,4},{6,5},{7,6},{0,7},{9,8},{10,9},{11,1... | collective-permute-start | bytes 884744 | tf_op jit(solution)/shard_map/ppermute | solution.py:18
  8.3 9.5 %collective-permute-done = bf16[4,9,32,128]{3,2,0,1:T(8,128)(2,1)S(1)} collective-permute-done((bf16[4,9,32,128]{3,2,0,1:T(8,128)(2,1)S(1)}, bf16[4,9,32,128]{3,2,0,1:T(8,128)(2,1)S(1)}, u32[]{:S(2)}, u32[]{:S(2)}) %collective-permute-start) | collective-permute-done | bytes 294944 | tf_op jit(solution)/shard_map/ppermute | solution.py:15
  17.8 2.2 %collective-permute-done.1 = bf16[4,9,32,128]{3,2,0,1:T(8,128)(2,1)S(1)} collective-permute-done((bf16[4,9,32,128]{3,2,0,1:T(8,128)(2,1)S(1)}, bf16[4,9,32,128]{3,2,0,1:T(8,128)(2,1)S(1)}, u32[]{:S(2)}, u32[]{:S(2)}) %collective-permute-start.1) | collective-permute-done | bytes 294944 | tf_op jit(solution)/shard_map/ppermute | solution.py:18
  21.2 1.7 collective-permute-start.3
  22.9 28.2 %collective-permute-done.2 = bf16[18,9,32,128]{3,2,0,1:T(8,128)(2,1)} collective-permute-done((bf16[18,9,32,128]{3,2,0,1:T(8,128)(2,1)}, bf16[18,9,32,128]{3,2,0,1:T(8,128)(2,1)}, u32[]{:S(2)}, u32[]{:S(2)}) %collective-permute-start.2) | collective-permute-done | bytes 1327136 | tf_op jit(solution)/shard_map/ppermute | solution.py:59
  51.2 1.3 broadcast.23.clone
  52.9 1.7 copy_dynamic-update-slice_fusion.6
  54.6 1.7 copy_dynamic-update-slice_fusion.5
  56.3 12.4 %collective-permute-done.4 = bf16[18,9,32,128]{3,2,0,1:T(8,128)(2,1)} collective-permute-done((bf16[18,9,32,128]{3,2,0,1:T(8,128)(2,1)}, bf16[18,9,32,128]{3,2,0,1:T(8,128)(2,1)}, u32[]{:S(2)}, u32[]{:S(2)}) %collective-permute-start.4) | collective-permute-done | bytes 1327136 | tf_op jit(solution)/shard_map/ppermute | solution.py:59
  68.7 1.6 copy_dynamic-update-slice_fusion.4
  70.3 9.0 %pad_slice_fusion.14 = (bf16[10,9,128,128]{3,2,1,0:T(8,128)(2,1)}, bf16[10,9,128,128]{3,2,1,0:T(8,128)(2,1)S(1)}, bf16[10,9,128,128]{3,2,1,0:T(8,128)(2,1)S(1)},...) fusion(bf16[18,9,128,128]{3,2,1,0:T(8,128)(2,1)S(1)} %copy_dyna, ...), kind=kLoop, calls=%fused_computation.14 | loop fusion | bytes 34799616 | tf_op jit(solution)/shard_map/slice | solution.py:31
  81.6 1.7 fusion.60
  84.0 1.7 fusion.64
  85.7 1.7 fusion.68
  87.4 1.7 fusion.40
  89.1 4.7 %fusion.84 = bf16[10,9,32,128]{3,2,0,1:T(8,128)(2,1)} fusion(bf16[10,9,128,128]{3,2,1,0:T(8,128)(2,1)S(1)} %get-tuple-element.20, f32[10,9,128,32]{2,3,0,1:T(8,128)} %fusion.40, f32[10,9,128,32]{2,3,0,1:T(8,128)S(1)} %fusion.44, f32[10,9,128,32]{2,3,0,1:T(8,128)S(1)} %fusion.48, f32[10,9,128,32]{2,3,0,1:T(8,128)S(1)} %fusion.52, ...), kind=kOutput, calls=%fused_computation.106 | convolution fusion | flops 98058240 | bytes 15566848 | tf_op jit(solution)/shard_map/rab,rwbc->rwac/dot_general | solution.py:34
  93.8 1.5 fusion.66
  99.3 2.1 %fusion.75 = bf16[10,9,32,128]{3,2,0,1:T(8,128)(2,1)S(1)} fusion(f32[10,9,128,32]{2,3,0,1:T(8,128)S(1)} %fusion.42, f32[10,9,128,32]{2,3,0,1:T(8,128)S(1)} %fusion.46, f32[10,9,128,32]{2,3,0,1:T(8,128)S(1)} %fusion.50, f32[10,9,128,32]{2,3,0,1:T(8,128)S(1)} %fusion.54, f32[10,9,128,32]{2,3,0,1:T(8,128)S(1)} %fusion.58, f32[10,9,128,32]{2,3,0,1:T(8,128)S(1)} %fusion.62, ...), kind=kOutput, calls=%fused_computation.93 | convolution fusion | flops 100270080 | bytes 16306180 | tf_op jit(solution)/shard_map/rab,rwbc->rwac/dot_general | solution.py:34
  101.8 4.4 %collective-permute-start.6 = (bf16[4,9,32,128]{3,2,0,1:T(8,128)(2,1)S(1)}, bf16[4,9,32,128]{3,2,0,1:T(8,128)(2,1)S(1)}, u32[]{:S(2)}, u32[]{:S(2)}) collective-permute-start(bf16[4,9,32,128]{3,2,0,1:T(8,128)(2,1)S(1)} %get-tuple-element.24), channel_id=1, source_target_pairs={{1,0},{2,1},{3,2},{4,3},{5,4},{6,5},{7,6},{0,7},{9,8},{10,9},{11,1... | collective-permute-start | bytes 884744 | tf_op jit(solution)/shard_map/ppermute | solution.py:18
  106.3 8.4 %collective-permute-done.5 = bf16[4,9,32,128]{3,2,0,1:T(8,128)(2,1)S(1)} collective-permute-done((bf16[4,9,32,128]{3,2,0,1:T(8,128)(2,1)S(1)}, bf16[4,9,32,128]{3,2,0,1:T(8,128)(2,1)S(1)}, u32[]{:S(2)}, u32[]{:S(2)}) %collective-permute-start.5) | collective-permute-done | bytes 294944 | tf_op jit(solution)/shard_map/ppermute | solution.py:15
  114.7 2.9 %collective-permute-done.6 = bf16[4,9,32,128]{3,2,0,1:T(8,128)(2,1)S(1)} collective-permute-done((bf16[4,9,32,128]{3,2,0,1:T(8,128)(2,1)S(1)}, bf16[4,9,32,128]{3,2,0,1:T(8,128)(2,1)S(1)}, u32[]{:S(2)}, u32[]{:S(2)}) %collective-permute-start.6) | collective-permute-done | bytes 294944 | tf_op jit(solution)/shard_map/ppermute | solution.py:18
  117.7 1.7 collective-permute-start.8
  119.5 29.6 %collective-permute-done.7 = bf16[18,9,32,128]{3,2,0,1:T(8,128)(2,1)S(1)} collective-permute-done((bf16[18,9,32,128]{3,2,0,1:T(8,128)(2,1)S(1)}, bf16[18,9,32,128]{3,2,0,1:T(8,128)(2,1)S(1)}, u32[]{:S(2)}, u32[]{:S(2)}) %collective-permute-start.7) | collective-permute-done | bytes 1327136 | tf_op jit(solution)/shard_map/ppermute | solution.py:59
  149.0 1.3 broadcast.23
  151.4 14.8 %collective-permute-done.9 = bf16[18,9,32,128]{3,2,0,1:T(8,128)(2,1)S(1)} collective-permute-done((bf16[18,9,32,128]{3,2,0,1:T(8,128)(2,1)S(1)}, bf16[18,9,32,128]{3,2,0,1:T(8,128)(2,1)S(1)}, u32[]{:S(2)}, u32[]{:S(2)}) %collective-permute-start.9) | collective-permute-done | bytes 1327136 | tf_op jit(solution)/shard_map/ppermute | solution.py:59
  166.6 8.2 %pad_slice_fusion.6 = (bf16[10,9,128,128]{3,2,1,0:T(8,128)(2,1)}, bf16[10,9,128,128]{3,2,1,0:T(8,128)(2,1)S(1)}, bf16[10,9,128,128]{3,2,1,0:T(8,128)(2,1)S(1)}, ...) fusion(bf16[18,9,128,128]{3,2,1,0:T(8,128)(2,1)S(1)} %copy_dyna, ...), kind=kLoop, calls=%fused_computation.6 | loop fusion | bytes 34799616 | tf_op jit(solution)/shard_map/slice | solution.py:31
  174.7 2.4 %fusion.28 = f32[10,9,128,32]{2,3,0,1:T(8,128)S(1)} fusion(bf16[10,9,128,128]{3,2,1,0:T(8,128)(2,1)} %get-tuple-element.5, bf16[10,9,32,128]{3,2,0,1:T(8,128)(2,1)S(1)} %fusion.75), kind=kOutput, calls=%fused_computation.44 | convolution fusion | flops 94371840 | bytes 4505600 | tf_op jit(solution)/shard_map/rab,rwbc->rwac/dot_general | solution.py:34
  179.9 1.7 fusion.8
  181.7 1.7 fusion.4
  183.3 4.0 %fusion.87 = bf16[10,9,32,128]{3,2,0,1:T(8,128)(2,1)} fusion(bf16[10,9,128,128]{3,2,1,0:T(8,128)(2,1)S(1)} %get-tuple-element.11, f32[10,9,128,32]{2,3,0,1:T(8,128)} %fusion.4, f32[10,9,128,32]{2,3,0,1:T(8,128)} %fusion.8, f32[10,9,128,32]{2,3,0,1:T(8,128)S(1)} %fusion.12, f32[10,9,128,32]{2,3,0,1:T(8,128)S(1)} %fusion.16, ...), kind=kOutput, calls=%fused_computation.107 | convolution fusion | flops 98058240 | bytes 15566848 | tf_op jit(solution)/shard_map/rab,rwbc->rwac/dot_general | solution.py:34
  187.3 1.5 fusion.30
  (62 shorter events, 21.4 us)
Async XLA Ops:
  0.0 1.8 copy-start
  2.1 17.9 %copy-start.5 = (bf16[10,9,32,128]{3,2,0,1:T(8,128)(2,1)}, bf16[10,9,32,128]{3,2,0,1:T(8,128)(2,1)S(1)}, u32[]{:S(2)}) copy-start(bf16[10,9,32,128]{3,2,0,1:T(8,128)(2,1)S(1)} %copy_select_fusion) | copy-start | bytes 2211844
  2.1 15.6 %collective-permute-start = (bf16[4,9,32,128]{3,2,0,1:T(8,128)(2,1)S(1)}, bf16[4,9,32,128]{3,2,0,1:T(8,128)(2,1)S(1)}, u32[]{:S(2)}, u32[]{:S(2)}) collective-permute-start(bf16[4,9,32,128]{3,2,0,1:T(8,128)(2,1)S(1)} %get-tuple-element.25), channel_id=1, source_target_pairs={{0,1},{1,2},{2,3},{3,4},{4,5},{5,6},{6,7},{7,0},{8,9},{9,10},{10,1... | collective-permute-start | bytes 884744 | tf_op jit(solution)/shard_map/ppermute | solution.py:15
  5.2 14.8 %collective-permute-start.1 = (bf16[4,9,32,128]{3,2,0,1:T(8,128)(2,1)S(1)}, bf16[4,9,32,128]{3,2,0,1:T(8,128)(2,1)S(1)}, u32[]{:S(2)}, u32[]{:S(2)}) collective-permute-start(bf16[4,9,32,128]{3,2,0,1:T(8,128)(2,1)S(1)} %get-tuple-element.26), channel_id=1, source_target_pairs={{1,0},{2,1},{3,2},{4,3},{5,4},{6,5},{7,6},{0,7},{9,8},{10,9},{11,1... | collective-permute-start | bytes 884744 | tf_op jit(solution)/shard_map/ppermute | solution.py:18
  21.2 30.0 %collective-permute-start.2 = (bf16[18,9,32,128]{3,2,0,1:T(8,128)(2,1)}, bf16[18,9,32,128]{3,2,0,1:T(8,128)(2,1)}, u32[]{:S(2)}, u32[]{:S(2)}) collective-permute-start(bf16[18,9,32,128]{3,2,0,1:T(8,128)(2,1)} %pad_maximum_fusion), channel_id=1, source_target_pairs={{0,8},{8,16},{16,24},{24,0},{1,9},{9,17},{17,25},{25,1},{2,10},{10... | collective-permute-start | bytes 3981320 | tf_op jit(solution)/shard_map/ppermute | solution.py:59
  21.2 33.4 %collective-permute-start.3 = (bf16[18,9,32,128]{3,2,0,1:T(8,128)(2,1)}, bf16[18,9,32,128]{3,2,0,1:T(8,128)(2,1)}, u32[]{:S(2)}, u32[]{:S(2)}) collective-permute-start(bf16[18,9,32,128]{3,2,0,1:T(8,128)(2,1)} %pad_maximum_fusion), channel_id=1, source_target_pairs={{0,24},{8,0},{16,8},{24,16},{1,25},{9,1},{17,9},{25,17},{2,26},{10... | collective-permute-start | bytes 3981320 | tf_op jit(solution)/shard_map/ppermute | solution.py:64
  51.2 17.5 %collective-permute-start.4 = (bf16[18,9,32,128]{3,2,0,1:T(8,128)(2,1)}, bf16[18,9,32,128]{3,2,0,1:T(8,128)(2,1)}, u32[]{:S(2)}, u32[]{:S(2)}) collective-permute-start(bf16[18,9,32,128]{3,2,0,1:T(8,128)(2,1)} %collective-permute-done.2), channel_id=1, source_target_pairs={{0,8},{8,16},{16,24},{24,0},{1,9},{9,17},{17,25},{25,1},{2,10},{10... | collective-permute-start | bytes 3981320 | tf_op jit(solution)/shard_map/ppermute | solution.py:59
  51.2 1.3 copy-start.6
  81.6 2.4 %copy-start.3 = (bf16[10,9,128,128]{3,2,1,0:T(8,128)(2,1)S(1)}, bf16[10,9,128,128]{3,2,1,0:T(8,128)(2,1)}, u32[]{:S(2)}) copy-start(bf16[10,9,128,128]{3,2,1,0:T(8,128)(2,1)} %get-tuple-element.14) | copy-start | bytes 8847364
  83.3 2.4 %copy-start.2 = (bf16[10,9,128,128]{3,2,1,0:T(8,128)(2,1)S(1)}, bf16[10,9,128,128]{3,2,1,0:T(8,128)(2,1)}, u32[]{:S(2)}) copy-start(bf16[10,9,128,128]{3,2,1,0:T(8,128)(2,1)} %get-tuple-element.22) | copy-start | bytes 8847364
  93.8 1.5 copy-start.8
  101.5 13.2 %collective-permute-start.5 = (bf16[4,9,32,128]{3,2,0,1:T(8,128)(2,1)S(1)}, bf16[4,9,32,128]{3,2,0,1:T(8,128)(2,1)S(1)}, u32[]{:S(2)}, u32[]{:S(2)}) collective-permute-start(bf16[4,9,32,128]{3,2,0,1:T(8,128)(2,1)S(1)} %get-tuple-element.23), channel_id=1, source_target_pairs={{0,1},{1,2},{2,3},{3,4},{4,5},{5,6},{6,7},{7,0},{8,9},{9,10},{10,1... | collective-permute-start | bytes 884744 | tf_op jit(solution)/shard_map/ppermute | solution.py:15
  101.8 15.7 %collective-permute-start.6 = (bf16[4,9,32,128]{3,2,0,1:T(8,128)(2,1)S(1)}, bf16[4,9,32,128]{3,2,0,1:T(8,128)(2,1)S(1)}, u32[]{:S(2)}, u32[]{:S(2)}) collective-permute-start(bf16[4,9,32,128]{3,2,0,1:T(8,128)(2,1)S(1)} %get-tuple-element.24), channel_id=1, source_target_pairs={{1,0},{2,1},{3,2},{4,3},{5,4},{6,5},{7,6},{0,7},{9,8},{10,9},{11,1... | collective-permute-start | bytes 884744 | tf_op jit(solution)/shard_map/ppermute | solution.py:18
  117.7 31.4 %collective-permute-start.7 = (bf16[18,9,32,128]{3,2,0,1:T(8,128)(2,1)S(1)}, bf16[18,9,32,128]{3,2,0,1:T(8,128)(2,1)S(1)}, u32[]{:S(2)}, u32[]{:S(2)}) collective-permute-start(bf16[18,9,32,128]{3,2,0,1:T(8,128)(2,1)S(1)} %pad_maximum_fusion.1), channel_id=1, source_target_pairs={{0,8},{8,16},{16,24},{24,0},{1,9},{9,17},{17,25},{25,1},{2,10},{10... | collective-permute-start | bytes 3981320 | tf_op jit(solution)/shard_map/ppermute | solution.py:59
  117.7 33.3 %collective-permute-start.8 = (bf16[18,9,32,128]{3,2,0,1:T(8,128)(2,1)S(1)}, bf16[18,9,32,128]{3,2,0,1:T(8,128)(2,1)S(1)}, u32[]{:S(2)}, u32[]{:S(2)}) collective-permute-start(bf16[18,9,32,128]{3,2,0,1:T(8,128)(2,1)S(1)} %pad_maximum_fusion.1), channel_id=1, source_target_pairs={{0,24},{8,0},{16,8},{24,16},{1,25},{9,1},{17,9},{25,17},{2,26},{10... | collective-permute-start | bytes 3981320 | tf_op jit(solution)/shard_map/ppermute | solution.py:64
  149.0 17.2 %collective-permute-start.9 = (bf16[18,9,32,128]{3,2,0,1:T(8,128)(2,1)S(1)}, bf16[18,9,32,128]{3,2,0,1:T(8,128)(2,1)S(1)}, u32[]{:S(2)}, u32[]{:S(2)}) collective-permute-start(bf16[18,9,32,128]{3,2,0,1:T(8,128)(2,1)S(1)} %collective-permute-done.7), channel_id=1, source_target_pairs={{0,8},{8,16},{16,24},{24,0},{1,9},{9,17},{17,25},{25,1},{2,10},{10... | collective-permute-start | bytes 3981320 | tf_op jit(solution)/shard_map/ppermute | solution.py:59
  183.3 4.0 %copy-start.4 = (bf16[10,9,128,128]{3,2,1,0:T(8,128)(2,1)S(1)}, bf16[10,9,128,128]{3,2,1,0:T(8,128)(2,1)}, u32[]{:S(2)}) copy-start(bf16[10,9,128,128]{3,2,1,0:T(8,128)(2,1)} %get-tuple-element.5) | copy-start | bytes 8847364
  187.3 1.5 copy-start.7
  192.8 2.1 %copy-start.1 = (bf16[10,9,128,128]{3,2,1,0:T(8,128)(2,1)S(1)}, bf16[10,9,128,128]{3,2,1,0:T(8,128)(2,1)}, u32[]{:S(2)}) copy-start(bf16[10,9,128,128]{3,2,1,0:T(8,128)(2,1)} %param.2) | copy-start | bytes 8847364
